TPU v7x, 32 devices: a whole 2x2x4 slice. The times are simulated.
32 devices in a mesh: rep: 8 (over z, y), tp: 4 (over x, core).
Axes of the slice: x: 2, y: 2, z: 4, core: 2. Of those that a mesh axis runs over, the one named last changes fastest.
Arguments:
- image_grads: bfloat16 [32, 48, 1280], P('rep', 'tp'), may hold values from -6 to 6
- dest_rank: int32 [32], P('rep'), may hold values from 0 to 7, as said below
- dest_slot: int32 [32], P('rep'), may hold values from 0 to 7, as said below
- saved_inputs: bfloat16 [64, 48, 1280], P('rep'), may hold values from -6 to 6
- up_weight: bfloat16 [1280, 5120], P(None, 'tp'), may hold values from -0.15625 to 0.15625
- down_weight: bfloat16 [5120, 1280], P('tp'), may hold values from -0.078125 to 0.078125
- norm_gain: float32 [1280], replicated, may hold values from 0.25 to 1.75
Outputs:
- input_grads: bfloat16 [64, 48, 1280], P('rep', 'tp')
- up_grads: float32 [1280, 5120], P('rep', 'tp')
- down_grads: float32 [5120, 1280], P('tp', 'rep')
- gain_grads: float32 [1280], replicated
Inputs may be any that keep to these rules, and one draw needn't show every extreme that they name: `dest_rank`: the images of one index of rep go to different owners; each owner receives at most 8 images, and some owner receives exactly 8 in every draw. `dest_slot`: the images that one owner receives have distinct slots 0, 1, ... up to their count less one; other slots hold no image.
All inputs are finite; a program needn't handle non-finite values.
Results may differ from a plain program's by a relative error of at most 0.015.
Values may be sent and summed in bfloat16 or wider, within the bound.
No kernel may reach another device: no remote copies, remote signals or barrier semaphores. Data moves between devices by JAX's collectives and lax.ppermute only.
A program may use at most 128 MiB of HBM per device.

v0:
```python
import jax
import jax.numpy as jnp
from jax import lax
from jax.sharding import PartitionSpec as P

epsilon = 1e-05
gelu_c = 0.7978845608028654
gelu_a = 0.044715


def gelu_value(preact):
    inner = jnp.tanh(gelu_c * (preact + gelu_a * preact**3))
    return 0.5 * preact * (1.0 + inner)


def gelu_slope(preact):
    inner = jnp.tanh(gelu_c * (preact + gelu_a * preact**3))
    return 0.5 * (1.0 + inner) + 0.5 * preact * (1.0 - inner * inner) * gelu_c * (
        1.0 + 3.0 * gelu_a * preact * preact
    )


def outbound(images, dest_rank, dest_slot, groups, capacity):
    rank_ids = jnp.arange(groups, dtype=jnp.int32)
    one_hot = dest_rank[None, :] == rank_ids[:, None]
    packed = jnp.einsum(
        "ek,kpd->epd", one_hot.astype(jnp.bfloat16), images, preferred_element_type=jnp.float32
    ).astype(jnp.bfloat16)
    present = jnp.any(one_hot, axis=1)
    slot_sent = jnp.sum(jnp.where(one_hot, dest_slot[None, :], 0), axis=1) + jnp.where(
        present, 0, capacity
    )
    return (packed, slot_sent)


def compact(inbound, slot_recv, capacity):
    slot_ids = jnp.arange(capacity, dtype=jnp.int32)
    picker = (slot_recv[None, :] == slot_ids[:, None]).astype(jnp.bfloat16)
    return jnp.einsum("ce,epd->cpd", picker, inbound, preferred_element_type=jnp.float32).astype(
        jnp.bfloat16
    )


def local(image_grads, dest_rank, dest_slot, saved_inputs, up_weight, down_weight, norm_gain):
    groups = lax.axis_size("rep")
    capacity = saved_inputs.shape[0]
    patches = saved_inputs.shape[1]
    width = saved_inputs.shape[2]
    slab = image_grads.shape[1]
    packed, slot_sent = outbound(image_grads, dest_rank, dest_slot, groups, capacity)
    inbound, slot_recv = (
        lax.all_to_all(packed, "rep", split_axis=0, concat_axis=0, tiled=True),
        lax.all_to_all(slot_sent, "rep", split_axis=0, concat_axis=0, tiled=True),
    )
    routed = lax.all_gather(compact(inbound, slot_recv, capacity), "tp", axis=1, tiled=True)
    rows = capacity * patches
    grads = routed.reshape(rows, width)
    values = saved_inputs.reshape(rows, width).astype(jnp.float32)
    mean_v = jnp.mean(values, axis=1, keepdims=True)
    var_v = jnp.mean((values - mean_v) ** 2, axis=1, keepdims=True)
    inv_std = 1.0 / jnp.sqrt(var_v + epsilon)
    centred = (values - mean_v) * inv_std
    normed = (centred * norm_gain[None, :]).astype(jnp.bfloat16)
    preact = jnp.dot(normed, up_weight, preferred_element_type=jnp.float32)
    hidden = gelu_value(preact).astype(jnp.bfloat16)
    grad_hidden = jnp.dot(grads, down_weight.T, preferred_element_type=jnp.float32)
    grad_pre = (grad_hidden * gelu_slope(preact)).astype(jnp.bfloat16)
    down_local = jnp.dot(hidden.T, grads, preferred_element_type=jnp.float32)
    up_local = jnp.dot(normed.T, grad_pre, preferred_element_type=jnp.float32)
    partial_normed = jnp.dot(grad_pre, up_weight.T, preferred_element_type=jnp.float32)
    up_grads, down_grads = (
        lax.psum_scatter(
            up_local.astype(jnp.bfloat16), "rep", scatter_dimension=0, tiled=True
        ).astype(jnp.float32),
        lax.psum_scatter(
            down_local.astype(jnp.bfloat16), "rep", scatter_dimension=1, tiled=True
        ).astype(jnp.float32),
    )
    start = lax.axis_index("tp") * slab
    grad_normed = lax.psum(partial_normed.astype(jnp.bfloat16), "tp").astype(jnp.float32)
    gain_grads = lax.psum(jnp.sum(grad_normed * centred, axis=0), "rep")
    scaled = grad_normed * norm_gain[None, :]
    first = jnp.mean(scaled, axis=1, keepdims=True)
    second = jnp.mean(scaled * centred, axis=1, keepdims=True)
    result = grads.astype(jnp.float32) + inv_std * (scaled - first - centred * second)
    result = result.reshape(capacity, patches, width)
    input_grads = lax.dynamic_slice_in_dim(result, start, slab, 1).astype(jnp.bfloat16)
    return (input_grads, up_grads, down_grads, gain_grads)


def solution(mesh):
    in_specs = (
        P("rep", "tp", None),
        P("rep"),
        P("rep"),
        P("rep", None, None),
        P(None, "tp"),
        P("tp", None),
        P(),
    )
    out_specs = (P("rep", "tp", None), P("rep", "tp"), P("tp", "rep"), P())
    return jax.shard_map(local, mesh=mesh, in_specs=in_specs, out_specs=out_specs, check_vma=False)
```

profile of v0, /device:TPU:0, one launch (start us, length us, event | category | flops | bytes accessed | tf_op | source)
XLA Modules:
  0.0 227.4 jit_solution(4812168266985921151)
XLA Ops:
  8.0 0.9 fusion.26
  8.9 0.9 select_reduce_fusion
  10.5 7.3 %all-to-all-start = ((s32[8,1,1]{2,1,0:T(1,128)}), s32[8,1,1]{2,1,0:T(1,128)S(1)}, u32[]{:S(2)}, u32[]{:S(2)}) async-start(s32[8,1,1]{2,1,0:T(1,128)} %copy.19), calls=%async_computation | async-start | bytes 8192 | tf_op jit(solution)/shard_map/all_to_all | solution.py:53
  17.8 1.4 convert_reduce_fusion
  19.3 1.6 multiply_reduce_fusion
  21.4 2.5 %multiply_convert_fusion.1 = bf16[384,1280]{1,0:T(8,128)(2,1)} fusion(bf16[8,48,1280]{2,1,0:T(8,128)(2,1)} %param.10, f32[1280]{0:T(1024)S(1)} %copy-done.5, f32[384]{0:T(512)S(1)} %div.18, f32[384]{0:T(512)S(1)} %sqrt.6), kind=kLoop, calls=%fused_computation.29 | loop fusion | flops 2457600 | bytes 1974272 | tf_op jit(solution)/shard_map/convert_element_type | solution.py:63
  24.7 6.0 %all-to-all-start.1 = ((bf16[8,12,1280]{2,1,0:T(8,128)(2,1)}), bf16[8,12,1280]{2,1,0:T(8,128)(2,1)}, u32[]{:S(2)}, u32[]{:S(2)}) async-start(bf16[8,12,1280]{2,1,0:T(8,128)(2,1)} %copy.20), calls=%async_computation.1 | async-start | bytes 655360 | tf_op jit(solution)/shard_map/all_to_all | solution.py:52
  30.7 4.0 %fusion.33 = f32[384,1280]{1,0:T(8,128)} fusion(bf16[384,1280]{1,0:T(8,128)(2,1)} %multiply_convert_fusion.1, bf16[1280,1280]{1,0:T(8,128)(2,1)S(1)} %copy-done), kind=kOutput, calls=%fused_computation.56 | convolution fusion | flops 1258291200 | bytes 6225920 | tf_op jit(solution)/shard_map/dot_general | solution.py:64
  34.9 5.6 %all-to-all-done.1 = bf16[8,12,1280]{2,1,0:T(8,128)(2,1)} async-done(((bf16[8,12,1280]{2,1,0:T(8,128)(2,1)}), bf16[8,12,1280]{2,1,0:T(8,128)(2,1)}, u32[]{:S(2)}, u32[]{:S(2)}) %all-to-all-start.1) | async-done | bytes 245792 | tf_op jit(solution)/shard_map/all_to_all | solution.py:52
  40.5 1.3 convolution_convert_fusion.3
  41.9 9.7 %all_gather.3 = bf16[8,48,1280]{2,0,1:T(8,128)(2,1)S(1)} all-gather(bf16[8,12,1280]{2,0,1:T(8,128)(2,1)S(1)} %convolution_convert_fusion.3), channel_id=1, replica_groups=mesh['rep'=8,'tp'=4] {'tp'}, dimensions={1}, use_global_device_ids=true | all-gather | bytes 1228800 | tf_op jit(solution)/shard_map/all_gather | solution.py:55
  51.7 3.8 %fusion = bf16[384,1280]{1,0:T(8,128)(2,1)S(1)} fusion(bf16[384,1280]{1,0:T(8,128)(2,1)S(1)} %bitcast.33, bf16[1280,1280]{1,0:T(8,128)(2,1)S(1)} %copy-done.7, f32[384,1280]{1,0:T(8,128)} %fusion.33), kind=kOutput, calls=%fused_computation.5 | convolution fusion | flops 1267630080 | bytes 7208960 | tf_op jit(solution)/shard_map/dot_general | solution.py:66
  55.6 0.9 copy-done.8
  56.5 2.4 %convolution_convert_fusion.2 = bf16[384,1280]{1,0:T(8,128)(2,1)} fusion(bf16[384,1280]{1,0:T(8,128)(2,1)S(1)} %fusion, bf16[1280,1280]{1,0:T(8,128)(2,1)S(1)} %copy-done), kind=kOutput, calls=%fused_computation.6 | convolution fusion | flops 1258782720 | bytes 5242880 | tf_op jit(solution)/shard_map/dot_general | solution.py:70
  59.0 5.1 %convolution_convert_fusion.1 = bf16[1280,1280]{1,0:T(8,128)(2,1)} fusion(bf16[384,1280]{1,0:T(8,128)(2,1)} %multiply_convert_fusion.1, bf16[384,1280]{1,0:T(8,128)(2,1)} %copy-done.8), kind=kOutput, calls=%fused_computation.1 | convolution fusion | flops 1259929600 | bytes 5242880 | tf_op jit(solution)/shard_map/dot_general | solution.py:69
  64.4 5.5 %convolution_convert_fusion = bf16[1280,1280]{0,1:T(8,128)(2,1)} fusion(bf16[384,1280]{1,0:T(8,128)(2,1)} %bitcast.34, f32[384,1280]{1,0:T(8,128)} %fusion.33), kind=kOutput, calls=%fused_computation | convolution fusion | flops 1264353280 | bytes 6225920 | tf_op jit(solution)/shard_map/dot_general | solution.py:68
  69.9 23.6 %all-reduce.2.cloned.1.call-done = bf16[384,1280]{1,0:T(8,128)(2,1)} async-done(((bf16[384,1280]{1,0:T(8,128)(2,1)}), bf16[384,1280]{1,0:T(8,128)(2,1)}) %all-reduce.2.cloned.1.call-update) | async-done | bytes 983056 | tf_op jit(solution)/shard_map/psum | solution.py:80
  93.5 2.6 %fusion.8 = (f32[1280]{0:T(1024)S(1)}, f32[384]{0:T(512)S(1)}, f32[384]{0:T(512)S(1)}) fusion(bf16[384,1280]{1,0:T(8,128)(2,1)} %all-reduce.2.cloned.1.call-done, bf16[8,48,1280]{2,1,0:T(8,128)(2,1)} %param.10, f32[384]{0:T(512)S(1)} %div.18, f32[384]{0:T(512)S(1)} %sqrt.6, f32[1280]{0:T(1024)S(1)} %copy-done.5), kind=kLoop, calls=%fused_computation.18 | loop fusion | flops 4913152 | bytes 1982464 | tf_op jit(solution)/shard_map/reduce_sum | solution.py:81
  96.1 2.1 fusion.6
  99.0 22.1 %psum.15 = f32[1280]{0:T(1024)} all-reduce(f32[1280]{0:T(1024)S(1)} %get-tuple-element.4), channel_id=1, replica_groups=mesh['rep'=8,'tp'=4] {'rep'}, use_global_device_ids=true, to_apply=%region_10.11 | all-reduce | flops 1280 | bytes 10240 | tf_op jit(solution)/shard_map/psum | solution.py:81
  121.2 18.0 %reduce-scatter.3.cloned.1.call-done = bf16[160,1280]{1,0:T(8,128)(2,1)} async-done(((bf16[1280,1280]{1,0:T(8,128)(2,1)}), bf16[160,1280]{1,0:T(8,128)(2,1)}) %reduce-scatter.3.cloned.1.call-update) | async-done | bytes 409616 | tf_op jit(solution)/shard_map/reduce_scatter | solution.py:72
  139.2 1.9 convert_element_type.63
  141.1 76.9 %reduce-scatter.5.cloned.1.call-done = bf16[1280,160]{0,1:T(8,128)(2,1)} async-done(((bf16[1280,1280]{0,1:T(8,128)(2,1)}), bf16[1280,160]{0,1:T(8,128)(2,1)}) %reduce-scatter.5.cloned.1.call-update) | async-done | bytes 409616 | tf_op jit(solution)/shard_map/reduce_scatter | solution.py:75
  218.0 1.9 convert_element_type.66
  (37 shorter events, 3.6 us)
Async XLA Ops:
  8.0 22.7 %copy-start = (bf16[1280,1280]{1,0:T(8,128)(2,1)S(1)}, bf16[1280,1280]{1,0:T(8,128)(2,1)}, u32[]{:S(2)}) copy-start(bf16[1280,1280]{1,0:T(8,128)(2,1)} %param.11) | copy-start | bytes 9830404
  8.0 13.0 %copy-start.6 = (s32[4]{0:T(128)S(1)}, s32[4]{0:T(128)}, u32[]{:S(2)}) copy-start(s32[4]{0:T(128)} %param.8) | copy-start | bytes 52
  8.0 13.0 %copy-start.4 = (bf16[4,12,1280]{2,0,1:T(4,128)(2,1)S(1)}, bf16[4,12,1280]{2,0,1:T(4,128)(2,1)}, u32[]{:S(2)}) copy-start(bf16[4,12,1280]{2,0,1:T(4,128)(2,1)} %param.7) | copy-start | bytes 368644
  8.0 13.4 %copy-start.5 = (f32[1280]{0:T(1024)S(1)}, f32[1280]{0:T(1024)}, u32[]{:S(2)}) copy-start(f32[1280]{0:T(1024)} %param.13) | copy-start | bytes 15364
  10.5 14.2 %all-to-all-start = ((s32[8,1,1]{2,1,0:T(1,128)}), s32[8,1,1]{2,1,0:T(1,128)S(1)}, u32[]{:S(2)}, u32[]{:S(2)}) async-start(s32[8,1,1]{2,1,0:T(1,128)} %copy.19), calls=%async_computation | async-start | bytes 8192 | tf_op jit(solution)/shard_map/all_to_all | solution.py:53
  24.7 15.8 %all-to-all-start.1 = ((bf16[8,12,1280]{2,1,0:T(8,128)(2,1)}), bf16[8,12,1280]{2,1,0:T(8,128)(2,1)}, u32[]{:S(2)}, u32[]{:S(2)}) async-start(bf16[8,12,1280]{2,1,0:T(8,128)(2,1)} %copy.20), calls=%async_computation.1 | async-start | bytes 655360 | tf_op jit(solution)/shard_map/all_to_all | solution.py:52
  30.7 62.8 %all-reduce.2.cloned.1.call-start = ((), (), s32[]{:S(2)}) async-start(), calls=%async_computation.4 | async-start | bytes 1966080 | tf_op jit(solution)/shard_map/psum | solution.py:80
  40.5 11.2 %copy-start.7 = (bf16[1280,1280]{1,0:T(8,128)(2,1)S(1)}, bf16[1280,1280]{1,0:T(8,128)(2,1)}, u32[]{:S(2)}) copy-start(bf16[1280,1280]{1,0:T(8,128)(2,1)} %param.12) | copy-start | bytes 9830404
  51.7 3.9 %copy-start.2 = (bf16[8,48,1280]{2,1,0:T(8,128)(2,1)}, bf16[8,48,1280]{2,1,0:T(8,128)(2,1)S(1)}, u32[]{:S(2)}) copy-start(bf16[8,48,1280]{2,1,0:T(8,128)(2,1)S(1)} %copy.22) | copy-start | bytes 2949124
  55.6 1.0 copy-start.8
  59.0 80.2 %reduce-scatter.3.cloned.1.call-start = ((), (), s32[]{:S(2)}) async-start(), calls=%async_computation.5 | async-start | bytes 3686400 | tf_op jit(solution)/shard_map/reduce_scatter | solution.py:72
  64.1 153.9 %reduce-scatter.5.cloned.1.call-start = ((), (), s32[]{:S(2)}) async-start(), calls=%async_computation.6 | async-start | bytes 3686400 | tf_op jit(solution)/shard_map/reduce_scatter | solution.py:75
  93.5 2.6 %copy-start.1 = (bf16[8,48,1280]{2,1,0:T(8,128)(2,1)S(1)}, bf16[8,48,1280]{2,1,0:T(8,128)(2,1)}, u32[]{:S(2)}) copy-start(bf16[8,48,1280]{2,1,0:T(8,128)(2,1)} %param.10) | copy-start | bytes 2949124
  93.5 2.6 %copy-start.3 = (bf16[8,48,1280]{2,1,0:T(8,128)(2,1)S(1)}, bf16[8,48,1280]{2,1,0:T(8,128)(2,1)}, u32[]{:S(2)}) copy-start(bf16[8,48,1280]{2,1,0:T(8,128)(2,1)} %copy-done.2) | copy-start | bytes 2949124
Sparse Core Ops, SparseCore 0:
  59.1 34.3 all-reduce.1
Sparse Core Ops, SparseCore 1:
  64.2 74.9 reduce-scatter.2
  142.6 75.3 reduce-scatter.4
where the time goes:
time: 228 us; the launch traced here: 227 us
  waiting for transfers between devices  124 us (54%)
  blocking collectives  31.8 us (14%)
  matrix products  22.5 us (10%)
  other arithmetic  16.1 us (7%)
  between operations  15.7 us (7%)
  starting transfers between devices  13.6 us (6%)
  local copies, waits for them, and re-layouts  3.62 us (2%)
    reduce_scatter x1, waiting for transfers between devices, local(): lax.psum_scatter(down_local.astype(jnp.bfloat16), 'rep', scatter_dimensio...  76.9 us
    psum x1, waiting for transfers between devices, local(): lax.psum(partial_normed.astype(jnp.bfloat16), 'tp').astype(jnp.float32)  23.6 us
    psum x1, blocking collectives, local(): gain_grads = lax.psum(jnp.sum(grad_normed * centred, axis=0), 'rep')  22.1 us
    reduce_scatter x1, waiting for transfers between devices, local(): lax.psum_scatter(up_local.astype(jnp.bfloat16), 'rep', scatter_dimension=...  18 us
    all_gather x1, blocking collectives, local(): lax.all_gather(compact(inbound, slot_recv, capacity), 'tp', axis=1, tiled...  9.67 us
    all_to_all x1, starting transfers between devices, local(): lax.all_to_all(slot_sent, 'rep', split_axis=0, concat_axis=0, tiled=True)  7.31 us
    all_to_all x1, starting transfers between devices, local(): lax.all_to_all(packed, 'rep', split_axis=0, concat_axis=0, tiled=True)  6 us
    all_to_all x1, waiting for transfers between devices, local(): lax.all_to_all(packed, 'rep', split_axis=0, concat_axis=0, tiled=True)  5.58 us
  transfers between devices with their start and end apart: 5, of which 4 were waited for; matrix products, arithmetic and copies ran while one was open for 13% of the time, Pallas kernels for 0%

commit v1 on v0

--- a/solution.py
+++ b/solution.py
@@ -2,6 +2,7 @@
 import jax.numpy as jnp
 from jax import lax
 from jax.sharding import PartitionSpec as P
+from jax.lax import all_gather
 
 epsilon = 1e-05
 gelu_c = 0.7978845608028654
@@ -78,7 +79,9 @@
     )
     start = lax.axis_index("tp") * slab
     grad_normed = lax.psum(partial_normed.astype(jnp.bfloat16), "tp").astype(jnp.float32)
-    gain_grads = lax.psum(jnp.sum(grad_normed * centred, axis=0), "rep")
+    xs = jnp.sum(grad_normed * centred, axis=0)
+    r_now = all_gather(xs, "rep")
+    gain_grads = jnp.sum(r_now, axis=0)
     scaled = grad_normed * norm_gain[None, :]
     first = jnp.mean(scaled, axis=1, keepdims=True)
     second = jnp.mean(scaled * centred, axis=1, keepdims=True)

time: 228 us -> 228 us (level)
  waiting for transfers between devices: 124 us -> 115 us
  blocking collectives: 31.8 us -> 40.6 us
    all_gather x0 -> x1, blocking collectives: none -> 30.9 us  [local(): r_now = all_gather(xs, 'rep')]
    psum x1 -> x0, blocking collectives: 22.1 us -> none  [local(): gain_grads = lax.psum(jnp.sum(grad_normed * centred, axis=0), 'rep')]
    reduce_scatter x1, waiting for transfers between devices: 18 us -> 8.42 us  [local(): lax.psum_scatter(up_local.astype(jnp.bfloat16), 'rep', scatter_dimension=...]
where the time goes in v1:
time: 228 us; the launch traced here: 227 us
  waiting for transfers between devices  115 us (50%)
  blocking collectives  40.6 us (18%)
  matrix products  22.5 us (10%)
  other arithmetic  16.7 us (7%)
  between operations  15.7 us (7%)
  starting transfers between devices  13.6 us (6%)
  local copies, waits for them, and re-layouts  3.63 us (2%)
    reduce_scatter x1, waiting for transfers between devices, local(): lax.psum_scatter(down_local.astype(jnp.bfloat16), 'rep', scatter_dimensio...  77 us
    all_gather x1, blocking collectives, local(): r_now = all_gather(xs, 'rep')  30.9 us
    psum x1, waiting for transfers between devices, local(): lax.psum(partial_normed.astype(jnp.bfloat16), 'tp').astype(jnp.float32)  23.6 us
    all_gather x1, blocking collectives, local(): lax.all_gather(compact(inbound, slot_recv, capacity), 'tp', axis=1, tiled...  9.67 us
    reduce_scatter x1, waiting for transfers between devices, local(): lax.psum_scatter(up_local.astype(jnp.bfloat16), 'rep', scatter_dimension=...  8.42 us
    all_to_all x1, starting transfers between devices, local(): lax.all_to_all(slot_sent, 'rep', split_axis=0, concat_axis=0, tiled=True)  7.31 us
    all_to_all x1, starting transfers between devices, local(): lax.all_to_all(packed, 'rep', split_axis=0, concat_axis=0, tiled=True)  6 us
    all_to_all x1, waiting for transfers between devices, local(): lax.all_to_all(packed, 'rep', split_axis=0, concat_axis=0, tiled=True)  5.58 us
  transfers between devices with their start and end apart: 5, of which 4 were waited for; matrix products, arithmetic and copies ran while one was open for 13% of the time, Pallas kernels for 0%

profile of v1, /device:TPU:0, one launch (start us, length us, event | category | flops | bytes accessed | tf_op | source)
XLA Modules:
  0.0 227.4 jit_solution(13557352704063759172)
XLA Ops:
  8.0 0.9 fusion.26
  8.9 0.9 select_reduce_fusion
  10.5 7.3 %all-to-all-start = ((s32[8,1,1]{2,1,0:T(1,128)}), s32[8,1,1]{2,1,0:T(1,128)S(1)}, u32[]{:S(2)}, u32[]{:S(2)}) async-start(s32[8,1,1]{2,1,0:T(1,128)} %copy.19), calls=%async_computation | async-start | bytes 8192 | tf_op jit(solution)/shard_map/all_to_all | solution.py:54
  17.8 1.4 convert_reduce_fusion
  19.3 1.6 multiply_reduce_fusion
  21.4 2.5 %multiply_convert_fusion.1 = bf16[384,1280]{1,0:T(8,128)(2,1)} fusion(bf16[8,48,1280]{2,1,0:T(8,128)(2,1)} %param.10, f32[1280]{0:T(1024)S(1)} %copy-done.5, f32[384]{0:T(512)S(1)} %div.18, f32[384]{0:T(512)S(1)} %sqrt.6), kind=kLoop, calls=%fused_computation.29 | loop fusion | flops 2457600 | bytes 1974272 | tf_op jit(solution)/shard_map/convert_element_type | solution.py:64
  24.7 6.0 %all-to-all-start.1 = ((bf16[8,12,1280]{2,1,0:T(8,128)(2,1)}), bf16[8,12,1280]{2,1,0:T(8,128)(2,1)}, u32[]{:S(2)}, u32[]{:S(2)}) async-start(bf16[8,12,1280]{2,1,0:T(8,128)(2,1)} %copy.20), calls=%async_computation.1 | async-start | bytes 655360 | tf_op jit(solution)/shard_map/all_to_all | solution.py:53
  30.7 4.0 %fusion.33 = f32[384,1280]{1,0:T(8,128)} fusion(bf16[384,1280]{1,0:T(8,128)(2,1)} %multiply_convert_fusion.1, bf16[1280,1280]{1,0:T(8,128)(2,1)S(1)} %copy-done), kind=kOutput, calls=%fused_computation.56 | convolution fusion | flops 1258291200 | bytes 6225920 | tf_op jit(solution)/shard_map/dot_general | solution.py:65
  34.9 5.6 %all-to-all-done.1 = bf16[8,12,1280]{2,1,0:T(8,128)(2,1)} async-done(((bf16[8,12,1280]{2,1,0:T(8,128)(2,1)}), bf16[8,12,1280]{2,1,0:T(8,128)(2,1)}, u32[]{:S(2)}, u32[]{:S(2)}) %all-to-all-start.1) | async-done | bytes 245792 | tf_op jit(solution)/shard_map/all_to_all | solution.py:53
  40.5 1.3 convolution_convert_fusion.3
  41.9 9.7 %all_gather.9 = bf16[8,48,1280]{2,0,1:T(8,128)(2,1)S(1)} all-gather(bf16[8,12,1280]{2,0,1:T(8,128)(2,1)S(1)} %convolution_convert_fusion.3), channel_id=1, replica_groups=mesh['rep'=8,'tp'=4] {'tp'}, dimensions={1}, use_global_device_ids=true | all-gather | bytes 1228800 | tf_op jit(solution)/shard_map/all_gather | solution.py:56
  51.7 3.8 %fusion = bf16[384,1280]{1,0:T(8,128)(2,1)S(1)} fusion(bf16[384,1280]{1,0:T(8,128)(2,1)S(1)} %bitcast.33, bf16[1280,1280]{1,0:T(8,128)(2,1)S(1)} %copy-done.7, f32[384,1280]{1,0:T(8,128)} %fusion.33), kind=kOutput, calls=%fused_computation.5 | convolution fusion | flops 1267630080 | bytes 7208960 | tf_op jit(solution)/shard_map/dot_general | solution.py:67
  55.6 0.9 copy-done.8
  56.5 2.4 %convolution_convert_fusion.2 = bf16[384,1280]{1,0:T(8,128)(2,1)} fusion(bf16[384,1280]{1,0:T(8,128)(2,1)S(1)} %fusion, bf16[1280,1280]{1,0:T(8,128)(2,1)S(1)} %copy-done), kind=kOutput, calls=%fused_computation.6 | convolution fusion | flops 1258782720 | bytes 5242880 | tf_op jit(solution)/shard_map/dot_general | solution.py:71
  59.0 5.1 %convolution_convert_fusion.1 = bf16[1280,1280]{1,0:T(8,128)(2,1)} fusion(bf16[384,1280]{1,0:T(8,128)(2,1)} %multiply_convert_fusion.1, bf16[384,1280]{1,0:T(8,128)(2,1)} %copy-done.8), kind=kOutput, calls=%fused_computation.1 | convolution fusion | flops 1259929600 | bytes 5242880 | tf_op jit(solution)/shard_map/dot_general | solution.py:70
  64.4 5.5 %convolution_convert_fusion = bf16[1280,1280]{0,1:T(8,128)(2,1)} fusion(bf16[384,1280]{1,0:T(8,128)(2,1)} %bitcast.34, f32[384,1280]{1,0:T(8,128)} %fusion.33), kind=kOutput, calls=%fused_computation | convolution fusion | flops 1264353280 | bytes 6225920 | tf_op jit(solution)/shard_map/dot_general | solution.py:69
  69.9 23.6 %all-reduce.2.cloned.1.call-done = bf16[384,1280]{1,0:T(8,128)(2,1)} async-done(((bf16[384,1280]{1,0:T(8,128)(2,1)}), bf16[384,1280]{1,0:T(8,128)(2,1)}) %all-reduce.2.cloned.1.call-update) | async-done | bytes 983056 | tf_op jit(solution)/shard_map/psum | solution.py:81
  93.5 2.6 %fusion.8 = (f32[1280]{0:T(1024)S(1)}, f32[384]{0:T(512)S(1)}, f32[384]{0:T(512)S(1)}) fusion(bf16[384,1280]{1,0:T(8,128)(2,1)} %all-reduce.2.cloned.1.call-done, bf16[8,48,1280]{2,1,0:T(8,128)(2,1)} %param.10, f32[384]{0:T(512)S(1)} %div.18, f32[384]{0:T(512)S(1)} %sqrt.6, f32[1280]{0:T(1024)S(1)} %copy-done.5), kind=kLoop, calls=%fused_computation.18 | loop fusion | flops 4913152 | bytes 1982464 | tf_op jit(solution)/shard_map/reduce_sum | solution.py:82
  96.1 2.1 fusion.6
  99.1 30.9 %all-gather.1 = f32[8,1,1280]{2,1,0:T(1,128)S(1)} all-gather(f32[1,1,1280]{2,1,0:T(1,128)S(1)} %reshape.87), channel_id=2, replica_groups=mesh['rep'=8,'tp'=4] {'rep'}, dimensions={0}, use_global_device_ids=true | all-gather | bytes 46080 | tf_op jit(solution)/shard_map/all_gather | solution.py:83
  130.6 8.4 %reduce-scatter.3.cloned.1.call-done = bf16[160,1280]{1,0:T(8,128)(2,1)} async-done(((bf16[1280,1280]{1,0:T(8,128)(2,1)}), bf16[160,1280]{1,0:T(8,128)(2,1)}) %reduce-scatter.3.cloned.1.call-update) | async-done | bytes 409616 | tf_op jit(solution)/shard_map/reduce_scatter | solution.py:73
  139.0 1.9 convert_element_type.63
  141.0 77.0 %reduce-scatter.5.cloned.1.call-done = bf16[1280,160]{0,1:T(8,128)(2,1)} async-done(((bf16[1280,1280]{0,1:T(8,128)(2,1)}), bf16[1280,160]{0,1:T(8,128)(2,1)}) %reduce-scatter.5.cloned.1.call-update) | async-done | bytes 409616 | tf_op jit(solution)/shard_map/reduce_scatter | solution.py:76
  218.0 1.9 convert_element_type.66
  (39 shorter events, 4.3 us)
Async XLA Ops:
  8.0 22.7 %copy-start = (bf16[1280,1280]{1,0:T(8,128)(2,1)S(1)}, bf16[1280,1280]{1,0:T(8,128)(2,1)}, u32[]{:S(2)}) copy-start(bf16[1280,1280]{1,0:T(8,128)(2,1)} %param.11) | copy-start | bytes 9830404
  8.0 13.0 %copy-start.6 = (s32[4]{0:T(128)S(1)}, s32[4]{0:T(128)}, u32[]{:S(2)}) copy-start(s32[4]{0:T(128)} %param.8) | copy-start | bytes 52
  8.0 13.0 %copy-start.4 = (bf16[4,12,1280]{2,0,1:T(4,128)(2,1)S(1)}, bf16[4,12,1280]{2,0,1:T(4,128)(2,1)}, u32[]{:S(2)}) copy-start(bf16[4,12,1280]{2,0,1:T(4,128)(2,1)} %param.7) | copy-start | bytes 368644
  8.0 13.4 %copy-start.5 = (f32[1280]{0:T(1024)S(1)}, f32[1280]{0:T(1024)}, u32[]{:S(2)}) copy-start(f32[1280]{0:T(1024)} %param.13) | copy-start | bytes 15364
  10.5 14.2 %all-to-all-start = ((s32[8,1,1]{2,1,0:T(1,128)}), s32[8,1,1]{2,1,0:T(1,128)S(1)}, u32[]{:S(2)}, u32[]{:S(2)}) async-start(s32[8,1,1]{2,1,0:T(1,128)} %copy.19), calls=%async_computation | async-start | bytes 8192 | tf_op jit(solution)/shard_map/all_to_all | solution.py:54
  24.7 15.8 %all-to-all-start.1 = ((bf16[8,12,1280]{2,1,0:T(8,128)(2,1)}), bf16[8,12,1280]{2,1,0:T(8,128)(2,1)}, u32[]{:S(2)}, u32[]{:S(2)}) async-start(bf16[8,12,1280]{2,1,0:T(8,128)(2,1)} %copy.20), calls=%async_computation.1 | async-start | bytes 655360 | tf_op jit(solution)/shard_map/all_to_all | solution.py:53
  30.7 62.8 %all-reduce.2.cloned.1.call-start = ((), (), s32[]{:S(2)}) async-start(), calls=%async_computation.4 | async-start | bytes 1966080 | tf_op jit(solution)/shard_map/psum | solution.py:81
  40.5 11.2 %copy-start.7 = (bf16[1280,1280]{1,0:T(8,128)(2,1)S(1)}, bf16[1280,1280]{1,0:T(8,128)(2,1)}, u32[]{:S(2)}) copy-start(bf16[1280,1280]{1,0:T(8,128)(2,1)} %param.12) | copy-start | bytes 9830404
  51.7 3.9 %copy-start.2 = (bf16[8,48,1280]{2,1,0:T(8,128)(2,1)}, bf16[8,48,1280]{2,1,0:T(8,128)(2,1)S(1)}, u32[]{:S(2)}) copy-start(bf16[8,48,1280]{2,1,0:T(8,128)(2,1)S(1)} %copy.22) | copy-start | bytes 2949124
  55.6 1.0 copy-start.8
  59.0 80.1 %reduce-scatter.3.cloned.1.call-start = ((), (), s32[]{:S(2)}) async-start(), calls=%async_computation.5 | async-start | bytes 3686400 | tf_op jit(solution)/shard_map/reduce_scatter | solution.py:73
  64.1 153.9 %reduce-scatter.5.cloned.1.call-start = ((), (), s32[]{:S(2)}) async-start(), calls=%async_computation.6 | async-start | bytes 3686400 | tf_op jit(solution)/shard_map/reduce_scatter | solution.py:76
  93.5 2.6 %copy-start.1 = (bf16[8,48,1280]{2,1,0:T(8,128)(2,1)S(1)}, bf16[8,48,1280]{2,1,0:T(8,128)(2,1)}, u32[]{:S(2)}) copy-start(bf16[8,48,1280]{2,1,0:T(8,128)(2,1)} %param.10) | copy-start | bytes 2949124
  93.5 2.6 %copy-start.3 = (bf16[8,48,1280]{2,1,0:T(8,128)(2,1)S(1)}, bf16[8,48,1280]{2,1,0:T(8,128)(2,1)}, u32[]{:S(2)}) copy-start(bf16[8,48,1280]{2,1,0:T(8,128)(2,1)} %copy-done.2) | copy-start | bytes 2949124
Sparse Core Ops, SparseCore 0:
  59.1 34.3 all-reduce.1
Sparse Core Ops, SparseCore 1:
  64.2 74.8 reduce-scatter.2
  142.5 75.4 reduce-scatter.4
